TPU v7x, 256 devices: a whole 4x4x8 slice. The times are simulated.
256 devices in a mesh: row: 16 (over z, core), col: 16 (over x, y).
Axes of the slice: x: 4, y: 4, z: 8, core: 2. Of those that a mesh axis runs over, the one named last changes fastest.
Arguments:
- gram: float32 [16, 16, 1024, 1024], P('row', 'col'), may hold values from -21834.348 to 21835.348, as said below
Outputs:
- factored: float32 [16, 16, 1024, 1024], P('row', 'col')
Inputs may be any that keep to these rules, and one draw needn't show every extreme that they name: gram holds a symmetric positive definite matrix of order 16384 whose smallest eigenvalue is at least 1.
All inputs are finite; a program needn't handle non-finite values.
Results may differ from a plain program's by a relative error of at most 0.0001.
Values sent between devices are 32-bit elements; how exact they have to be, the bound alone decides.
No kernel may reach another device: no remote copies, remote signals or barrier semaphores. Data moves between devices by JAX's collectives and lax.ppermute only.
A program may use at most 64 MiB of HBM per device.

v0:
```python
import jax
import jax.numpy as jnp
from jax import lax
from jax.sharding import Mesh
from jax.sharding import PartitionSpec as P

BS = 256
PANELS = 3
ROW = ("row_0", "row_1")


def broadcast(shard, axis, root):
    return lax.dynamic_index_in_dim(lax.all_gather(shard, axis), root, 0, keepdims=False)


def spread(shard, axis, root):
    mine = lax.axis_index(axis) == root
    return lax.psum(jnp.where(mine, shard, jnp.zeros_like(shard)), axis)


def rows_for(lines, devices):
    spare = -len(lines) % devices
    return jnp.pad(lines, [(0, spare)] + [(0, 0)] * (lines.ndim - 1))


def own_block(blocks, axes, sequence):
    inside = blocks.shape[1:]
    blocks = blocks.reshape(*(lax.axis_size(a) for a in axes), *inside)
    blocks = jnp.moveaxis(blocks, sequence, range(len(axes))).reshape(-1, *inside)
    for k in sequence:
        blocks = lax.psum_scatter(blocks, axes[k], scatter_dimension=0, tiled=True)
    return blocks[0]


def stacked_from(shard, axes, sequence):
    blocks = shard[None]
    for k in sequence:
        blocks = lax.all_gather(blocks, axes[k], axis=0, tiled=True)
    current = [lax.axis_size(axes[k]) for k in reversed(sequence)]
    blocks = blocks.reshape(*current, *shard.shape)
    turned = sorted(range(len(sequence)), key=lambda place: sequence[len(sequence) - 1 - place])
    return blocks.transpose(*turned, *range(len(sequence), blocks.ndim)).reshape(-1, *shard.shape)


def total_of(shard, axes, sequence):
    devices, lines = (lax.axis_size(axes), shard.reshape(-1, *shard.shape[1:][-1:]))
    blocks = rows_for(lines, devices).reshape(devices, -1, *lines.shape[1:])
    own = own_block(blocks, axes, sequence)
    whole = stacked_from(own, axes, sequence[::-1]).reshape(-1, *lines.shape[1:])
    return whole[: len(lines)].reshape(shard.shape)


def full_dot(left, right):
    return jnp.dot(
        left, right.T, precision=lax.Precision.HIGHEST, preferred_element_type=jnp.float32
    )


def on_device(gram):
    matrix = gram[0, 0]
    grid_rows = lax.axis_size(ROW)
    grid_cols = lax.axis_size("col")
    own_row = lax.axis_index(ROW)
    own_col = lax.axis_index("col")
    row_count = matrix.shape[0] // BS
    col_count = matrix.shape[1] // BS
    row_blocks = jnp.repeat(jnp.arange(row_count, dtype=jnp.int32) * grid_rows + own_row, BS)
    col_blocks = jnp.repeat(jnp.arange(col_count, dtype=jnp.int32) * grid_cols + own_col, BS)
    for step in range(PANELS):
        first = step // grid_cols * BS
        column = matrix[:, first : first + BS]
        factor_first = step // grid_rows * BS
        corner = broadcast(column[factor_first : factor_first + BS], ROW, step % grid_rows)
        holder = own_col == step % grid_cols
        corner = jnp.where(holder, corner, jnp.eye(BS, dtype=jnp.float32))
        diagonal = jnp.linalg.cholesky(corner)
        solved = lax.linalg.triangular_solve(
            diagonal, column, left_side=False, lower=True, transpose_a=True
        )
        tiled = jnp.tile(diagonal, (row_count, 1))
        result = jnp.where((row_blocks == step)[:, None], tiled, solved)
        result = jnp.where((row_blocks < step)[:, None], jnp.zeros_like(result), result)
        panel_rows = spread(result, "col", step % grid_cols)
        wanted = jnp.arange(col_count, dtype=jnp.int32)[:, None] * grid_cols + own_col
        summed_present = jnp.arange(row_count, dtype=jnp.int32)[None, :] * grid_rows + own_row
        select = (wanted == summed_present).astype(jnp.float32)
        pieces = jnp.einsum(
            "ci,irs->crs",
            select,
            panel_rows.reshape(row_count, BS, BS),
            precision=lax.Precision.HIGHEST,
        )
        panel_cols = total_of(pieces.reshape(col_count * BS, BS), ROW, (0, 1))
        left = jnp.where((row_blocks > step)[:, None], panel_rows, jnp.zeros_like(panel_rows))
        right = jnp.where((col_blocks > step)[:, None], panel_cols, jnp.zeros_like(panel_cols))
        current = matrix - full_dot(left, right)
        finish_first = step // grid_cols * BS
        present = current[:, finish_first : finish_first + BS]
        current = current.at[:, finish_first : finish_first + BS].set(
            jnp.where(own_col == step % grid_cols, panel_rows, present)
        )
        cleared = (row_blocks == step)[:, None] & (col_blocks > step)[None, :]
        matrix = jnp.where(cleared, jnp.zeros_like(current), current)
    return matrix[None, None]


def solution(mesh):
    split = Mesh(mesh.devices.reshape(8, 2, mesh.shape["col"]), ("row_0", "row_1", "col"))
    return jax.shard_map(
        on_device,
        mesh=split,
        in_specs=(P(ROW, "col", None, None),),
        out_specs=P(ROW, "col", None, None),
        check_vma=False,
    )
```

profile of v0, /device:TPU:2, one launch (start us, length us, event | category | flops | bytes accessed | tf_op | source)
XLA Modules:
  0.0 979.8 jit_solution(14150500300622532511)
XLA Ops:
  6.5 5.3 copy.36
  11.9 1.7 slice.180
  13.8 45.0 %all-gather.16.cloned.1.call-done = f32[4096,256]{0,1:T(8,128)} async-done(((f32[256,256]{0,1:T(8,128)}), f32[4096,256]{0,1:T(8,128)}) %all-gather.16.cloned.1.call-update) | async-done | bytes 4194320 | tf_op jit(solution)/shard_map/all_gather | solution.py:13
  60.9 11.7 %cholesky.172 = f32[128,128]{1,0:T(8,128)S(1)} custom-call(f32[128,128]{1,0:T(8,128)S(1)} %cholesky.270), custom_call_target="Cholesky" | custom-call | tf_op jit(solution)/shard_map/jit(cholesky)/cholesky | solution.py:76
  72.7 9.8 %custom-call.15 = f32[1,128,128]{1,2,0:T(8,128)S(1)} custom-call(f32[1,128,128]{2,1,0:T(8,128)S(1)} %get-tuple-element.113), custom_call_target="InvertDiagBlocksLowerTriangular" | custom-call | tf_op jit(solution)/shard_map/jit(cholesky)/cholesky | solution.py:76
  83.0 11.7 %cholesky.189 = f32[128,128]{1,0:T(8,128)S(1)} custom-call(f32[128,128]{1,0:T(8,128)S(1)} %convolution_subtract_fusion.8), custom_call_target="Cholesky" | custom-call | tf_op jit(solution)/shard_map/jit(cholesky)/cholesky | solution.py:76
  96.9 4.4 while.9
  101.3 19.7 %custom-call.16 = f32[2,128,128]{1,2,0:T(8,128)S(1)} custom-call(f32[2,128,128]{2,1,0:T(8,128)S(1)} %get-tuple-element.63), custom_call_target="InvertDiagBlocksLowerTriangular" | custom-call | tf_op jit(solution)/shard_map/triangular_solve/custom-call.0 | solution.py:77
  121.0 1.7 fusion.19
  126.8 95.4 %all-reduce.5.cloned.1.call-done = f32[1024,256]{0,1:T(8,128)} async-done(((f32[1024,256]{0,1:T(8,128)}), f32[1024,256]{0,1:T(8,128)}) %all-reduce.5.cloned.1.call-update) | async-done | bytes 1048592 | tf_op jit(solution)/shard_map/psum | solution.py:18
  222.2 1.7 reshape.231
  227.0 38.5 %reduce-scatter.7.cloned.1.call-done = f32[2,64,256]{2,1,0:T(8,128)} async-done(((f32[16,64,256]{2,1,0:T(8,128)}), f32[2,64,256]{2,1,0:T(8,128)}) %reduce-scatter.7.cloned.1.call-update) | async-done | bytes 131088 | tf_op jit(solution)/shard_map/reduce_scatter | solution.py:31
  265.6 13.8 %reduce-scatter.9.cloned.1.call-done = f32[1,64,256]{2,1,0:T(8,128)} async-done(((f32[2,64,256]{2,1,0:T(8,128)}), f32[1,64,256]{2,1,0:T(8,128)}) %reduce-scatter.9.cloned.1.call-update) | async-done | bytes 65552 | tf_op jit(solution)/shard_map/reduce_scatter | solution.py:31
  279.4 3.5 all_gather.38
  283.8 39.3 %all-gather.10.cloned.1.call-done = f32[16,64,256]{2,1,0:T(8,128)} async-done(((f32[2,64,256]{2,1,0:T(8,128)}), f32[16,64,256]{2,1,0:T(8,128)}) %all-gather.10.cloned.1.call-update) | async-done | bytes 1048592 | tf_op jit(solution)/shard_map/all_gather | solution.py:38
  324.7 5.5 convolution_subtract_fusion.2
  331.6 2.0 copy-done.1
  335.0 40.1 %all-gather.18.cloned.1.call-done = f32[4096,256]{0,1:T(8,128)} async-done(((f32[256,256]{0,1:T(8,128)}), f32[4096,256]{0,1:T(8,128)}) %all-gather.18.cloned.1.call-update) | async-done | bytes 4194320 | tf_op jit(solution)/shard_map/all_gather | solution.py:13
  377.2 11.7 %cholesky.206 = f32[128,128]{1,0:T(8,128)S(1)} custom-call(f32[128,128]{1,0:T(8,128)S(1)} %cholesky.273), custom_call_target="Cholesky" | custom-call | tf_op jit(solution)/shard_map/jit(cholesky)/cholesky | solution.py:76
  389.0 9.8 %custom-call.17 = f32[1,128,128]{1,2,0:T(8,128)S(1)} custom-call(f32[1,128,128]{2,1,0:T(8,128)S(1)} %get-tuple-element.109), custom_call_target="InvertDiagBlocksLowerTriangular" | custom-call | tf_op jit(solution)/shard_map/jit(cholesky)/cholesky | solution.py:76
  399.3 11.7 %cholesky.223 = f32[128,128]{1,0:T(8,128)S(1)} custom-call(f32[128,128]{1,0:T(8,128)S(1)} %convolution_subtract_fusion.7), custom_call_target="Cholesky" | custom-call | tf_op jit(solution)/shard_map/jit(cholesky)/cholesky | solution.py:76
  413.8 4.3 while.10
  418.2 19.7 %custom-call.18 = f32[2,128,128]{1,2,0:T(8,128)S(1)} custom-call(f32[2,128,128]{2,1,0:T(8,128)S(1)} %get-tuple-element.64), custom_call_target="InvertDiagBlocksLowerTriangular" | custom-call | tf_op jit(solution)/shard_map/triangular_solve/custom-call.0 | solution.py:77
  437.8 1.7 fusion.17
  443.6 95.4 %all-reduce.7.cloned.1.call-done = f32[1024,256]{0,1:T(8,128)} async-done(((f32[1024,256]{0,1:T(8,128)}), f32[1024,256]{0,1:T(8,128)}) %all-reduce.7.cloned.1.call-update) | async-done | bytes 1048592 | tf_op jit(solution)/shard_map/psum | solution.py:18
  539.0 1.7 reshape.232
  543.9 38.5 %reduce-scatter.11.cloned.1.call-done = f32[2,64,256]{2,1,0:T(8,128)} async-done(((f32[16,64,256]{2,1,0:T(8,128)}), f32[2,64,256]{2,1,0:T(8,128)}) %reduce-scatter.11.cloned.1.call-update) | async-done | bytes 131088 | tf_op jit(solution)/shard_map/reduce_scatter | solution.py:31
  582.4 14.0 %reduce-scatter.13.cloned.1.call-done = f32[1,64,256]{2,1,0:T(8,128)} async-done(((f32[2,64,256]{2,1,0:T(8,128)}), f32[1,64,256]{2,1,0:T(8,128)}) %reduce-scatter.13.cloned.1.call-update) | async-done | bytes 65552 | tf_op jit(solution)/shard_map/reduce_scatter | solution.py:31
  596.4 3.5 all_gather.42
  600.2 39.9 %all-gather.12.cloned.1.call-done = f32[16,64,256]{2,1,0:T(8,128)} async-done(((f32[2,64,256]{2,1,0:T(8,128)}), f32[16,64,256]{2,1,0:T(8,128)}) %all-gather.12.cloned.1.call-update) | async-done | bytes 1048592 | tf_op jit(solution)/shard_map/all_gather | solution.py:38
  641.7 5.5 convolution_subtract_fusion.1
  648.6 2.0 copy-done
  651.9 40.3 %all-gather.20.cloned.1.call-done = f32[4096,256]{0,1:T(8,128)} async-done(((f32[256,256]{0,1:T(8,128)}), f32[4096,256]{0,1:T(8,128)}) %all-gather.20.cloned.1.call-update) | async-done | bytes 4194320 | tf_op jit(solution)/shard_map/all_gather | solution.py:13
  694.3 11.7 %cholesky.240 = f32[128,128]{1,0:T(8,128)S(1)} custom-call(f32[128,128]{1,0:T(8,128)S(1)} %cholesky.276), custom_call_target="Cholesky" | custom-call | tf_op jit(solution)/shard_map/jit(cholesky)/cholesky | solution.py:76
  706.0 9.8 %custom-call.19 = f32[1,128,128]{1,2,0:T(8,128)S(1)} custom-call(f32[1,128,128]{2,1,0:T(8,128)S(1)} %get-tuple-element.105), custom_call_target="InvertDiagBlocksLowerTriangular" | custom-call | tf_op jit(solution)/shard_map/jit(cholesky)/cholesky | solution.py:76
  716.3 11.7 %cholesky.257 = f32[128,128]{1,0:T(8,128)S(1)} custom-call(f32[128,128]{1,0:T(8,128)S(1)} %convolution_subtract_fusion.6), custom_call_target="Cholesky" | custom-call | tf_op jit(solution)/shard_map/jit(cholesky)/cholesky | solution.py:76
  730.9 4.4 while.11
  735.3 19.7 %custom-call.20 = f32[2,128,128]{1,2,0:T(8,128)S(1)} custom-call(f32[2,128,128]{2,1,0:T(8,128)S(1)} %get-tuple-element.65), custom_call_target="InvertDiagBlocksLowerTriangular" | custom-call | tf_op jit(solution)/shard_map/triangular_solve/custom-call.0 | solution.py:77
  755.0 1.7 fusion.15
  760.8 95.4 %all-reduce.9.cloned.1.call-done = f32[1024,256]{0,1:T(8,128)} async-done(((f32[1024,256]{0,1:T(8,128)}), f32[1024,256]{0,1:T(8,128)}) %all-reduce.9.cloned.1.call-update) | async-done | bytes 1048592 | tf_op jit(solution)/shard_map/psum | solution.py:18
  856.2 1.7 reshape.233
  861.0 38.5 %reduce-scatter.15.cloned.1.call-done = f32[2,64,256]{2,1,0:T(8,128)} async-done(((f32[16,64,256]{2,1,0:T(8,128)}), f32[2,64,256]{2,1,0:T(8,128)}) %reduce-scatter.15.cloned.1.call-update) | async-done | bytes 131088 | tf_op jit(solution)/shard_map/reduce_scatter | solution.py:31
  899.6 13.8 %reduce-scatter.17.cloned.1.call-done = f32[1,64,256]{2,1,0:T(8,128)} async-done(((f32[2,64,256]{2,1,0:T(8,128)}), f32[1,64,256]{2,1,0:T(8,128)}) %reduce-scatter.17.cloned.1.call-update) | async-done | bytes 65552 | tf_op jit(solution)/shard_map/reduce_scatter | solution.py:31
  913.4 3.5 all_gather.46
  917.1 40.0 %all-gather.14.cloned.1.call-done = f32[16,64,256]{2,1,0:T(8,128)} async-done(((f32[2,64,256]{2,1,0:T(8,128)}), f32[16,64,256]{2,1,0:T(8,128)}) %all-gather.14.cloned.1.call-update) | async-done | bytes 1048592 | tf_op jit(solution)/shard_map/all_gather | solution.py:38
  958.7 5.5 convolution_subtract_fusion
  965.1 2.4 select_bitcast_fusion
  967.5 5.3 copy.58
  (167 shorter events, 58.3 us)
Async XLA Ops:
  6.5 52.3 %all-gather.16.cloned.1.call-start = ((), (), s32[]{:S(2)}) async-start(), calls=%async_computation.18 | async-start | bytes 4456448 | tf_op jit(solution)/shard_map/all_gather | solution.py:13
  13.6 208.6 %all-reduce.5.cloned.1.call-start = ((), (), s32[]{:S(2)}) async-start(), calls=%async_computation.6 | async-start | bytes 2097152 | tf_op jit(solution)/shard_map/psum | solution.py:18
  126.7 138.8 %reduce-scatter.7.cloned.1.call-start = ((), (), s32[]{:S(2)}) async-start(), calls=%async_computation.7 | async-start | bytes 1179648 | tf_op jit(solution)/shard_map/reduce_scatter | solution.py:31
  224.6 100.1 %copy-start.2 = (f32[1024,256]{0,1:T(8,128)S(1)}, f32[1024,256]{0,1:T(8,128)}, u32[]{:S(2)}) copy-start(f32[1024,256]{0,1:T(8,128)} %all-reduce.5.cloned.1.call-done) | copy-start | bytes 3145732
  226.9 52.4 %reduce-scatter.9.cloned.1.call-start = ((), (), s32[]{:S(2)}) async-start(), calls=%async_computation.8 | async-start | bytes 196608 | tf_op jit(solution)/shard_map/reduce_scatter | solution.py:31
  265.5 57.6 %all-gather.10.cloned.1.call-start = ((), (), s32[]{:S(2)}) async-start(), calls=%async_computation.9 | async-start | bytes 1179648 | tf_op jit(solution)/shard_map/all_gather | solution.py:38
  282.9 92.2 %all-gather.18.cloned.1.call-start = ((), (), s32[]{:S(2)}) async-start(), calls=%async_computation.19 | async-start | bytes 4456448 | tf_op jit(solution)/shard_map/all_gather | solution.py:13
  331.6 2.0 copy-start.1
  334.3 204.7 %all-reduce.7.cloned.1.call-start = ((), (), s32[]{:S(2)}) async-start(), calls=%async_computation.10 | async-start | bytes 2097152 | tf_op jit(solution)/shard_map/psum | solution.py:18
  443.6 138.8 %reduce-scatter.11.cloned.1.call-start = ((), (), s32[]{:S(2)}) async-start(), calls=%async_computation.11 | async-start | bytes 1179648 | tf_op jit(solution)/shard_map/reduce_scatter | solution.py:31
  541.4 100.3 %copy-start.4 = (f32[1024,256]{0,1:T(8,128)S(1)}, f32[1024,256]{0,1:T(8,128)}, u32[]{:S(2)}) copy-start(f32[1024,256]{0,1:T(8,128)} %all-reduce.7.cloned.1.call-done) | copy-start | bytes 3145732
  543.8 52.6 %reduce-scatter.13.cloned.1.call-start = ((), (), s32[]{:S(2)}) async-start(), calls=%async_computation.12 | async-start | bytes 196608 | tf_op jit(solution)/shard_map/reduce_scatter | solution.py:31
  582.4 57.8 %all-gather.12.cloned.1.call-start = ((), (), s32[]{:S(2)}) async-start(), calls=%async_computation.13 | async-start | bytes 1179648 | tf_op jit(solution)/shard_map/all_gather | solution.py:38
  600.0 92.2 %all-gather.20.cloned.1.call-start = ((), (), s32[]{:S(2)}) async-start(), calls=%async_computation.20 | async-start | bytes 4456448 | tf_op jit(solution)/shard_map/all_gather | solution.py:13
  648.6 2.0 copy-start
  651.4 204.8 %all-reduce.9.cloned.1.call-start = ((), (), s32[]{:S(2)}) async-start(), calls=%async_computation.14 | async-start | bytes 2097152 | tf_op jit(solution)/shard_map/psum | solution.py:18
  760.7 138.8 %reduce-scatter.15.cloned.1.call-start = ((), (), s32[]{:S(2)}) async-start(), calls=%async_computation.15 | async-start | bytes 1179648 | tf_op jit(solution)/shard_map/reduce_scatter | solution.py:31
  858.6 100.1 %copy-start.3 = (f32[1024,256]{0,1:T(8,128)S(1)}, f32[1024,256]{0,1:T(8,128)}, u32[]{:S(2)}) copy-start(f32[1024,256]{0,1:T(8,128)} %all-reduce.9.cloned.1.call-done) | copy-start | bytes 3145732
  861.0 52.5 %reduce-scatter.17.cloned.1.call-start = ((), (), s32[]{:S(2)}) async-start(), calls=%async_computation.16 | async-start | bytes 196608 | tf_op jit(solution)/shard_map/reduce_scatter | solution.py:31
  899.5 57.6 %all-gather.14.cloned.1.call-start = ((), (), s32[]{:S(2)}) async-start(), calls=%async_computation.17 | async-start | bytes 1179648 | tf_op jit(solution)/shard_map/all_gather | solution.py:38
Sparse Core Ops, SparseCore 0:
  13.7 45.0 all-gather.15
  126.8 95.2 all-reduce.4
  227.1 38.3 reduce-scatter.6
  267.8 11.5 reduce-scatter.8
  283.0 39.9 all-gather.9
  334.5 40.5 all-gather.17
  443.7 95.2 all-reduce.6
  543.9 38.3 reduce-scatter.10
  584.8 11.5 reduce-scatter.12
  600.1 39.9 all-gather.11
  651.5 40.5 all-gather.19
  760.8 95.2 all-reduce.8
  861.1 38.3 reduce-scatter.14
  901.8 11.5 reduce-scatter.16
  917.1 39.9 all-gather.13
where the time goes:
time: 989 us; the launch traced here: 980 us
  waiting for transfers between devices  688 us (70%)
  other arithmetic  179 us (18%)
  local copies, waits for them, and re-layouts  48.8 us (5%)
  matrix products  33 us (3%)
  between operations  18.3 us (2%)
  blocking collectives  10.6 us (1%)
    psum x3, waiting for transfers between devices, spread(): return lax.psum(jnp.where(mine, shard, jnp.zeros_like(shard)), axis)  286 us
    reduce_scatter x6, waiting for transfers between devices, own_block(): blocks = lax.psum_scatter(blocks, axes[k], scatter_dimension=0, tiled=True)  157 us
    all_gather x3, waiting for transfers between devices, broadcast(): lax.all_gather(shard, axis)  125 us
    all_gather x3, waiting for transfers between devices, stacked_from(): blocks = lax.all_gather(blocks, axes[k], axis=0, tiled=True)  119 us
    another operation x20, other arithmetic, on_device(): diagonal = jnp.linalg.cholesky(corner)  103 us
    another operation x7, other arithmetic, on_device(): lax.linalg.triangular_solve(diagonal, column, left_side=False, lower=True...  59.1 us
  transfers between devices with their start and end apart: 15, of which 15 were waited for; matrix products, arithmetic and copies ran while one was open for 0% of the time, Pallas kernels for 0%

commit v1 on v0

--- a/solution.py
+++ b/solution.py
@@ -15,7 +15,7 @@
 
 def spread(shard, axis, root):
     mine = lax.axis_index(axis) == root
-    return lax.psum(jnp.where(mine, shard, jnp.zeros_like(shard)), axis)
+    return jnp.sum(lax.all_gather(jnp.where(mine, shard, jnp.zeros_like(shard)), axis), axis=0)
 
 
 def rows_for(lines, devices):

time: 989 us -> 1130 us (1.14)
  waiting for transfers between devices: 688 us -> 747 us
  local copies, waits for them, and re-layouts: 48.8 us -> 99.7 us
  other arithmetic: 179 us -> 208 us
    all_gather x0 -> x3, waiting for transfers between devices: none -> 345 us  [spread(): lax.all_gather(jnp.where(mine, shard, jnp.zeros_like(shard)), axis)]
    psum x3 -> x0, waiting for transfers between devices: 286 us -> none  [spread(): return lax.psum(jnp.where(mine, shard, jnp.zeros_like(shard)), axis)]
    unnamed x14 -> x11, local copies, waits for them, and re-layouts: 9.96 us -> 65.8 us
    reduce_sum x0 -> x3, other arithmetic: none -> 29.5 us  [spread(): jnp.sum(lax.all_gather(jnp.where(mine, shard, jnp.zeros_like(shard)), axi...]
where the time goes in v1:
time: 1130 us; the launch traced here: 1120 us
  waiting for transfers between devices  747 us (66%)
  other arithmetic  208 us (18%)
  local copies, waits for them, and re-layouts  99.7 us (9%)
  matrix products  33.4 us (3%)
  between operations  17.9 us (2%)
    all_gather x3, waiting for transfers between devices, spread(): lax.all_gather(jnp.where(mine, shard, jnp.zeros_like(shard)), axis)  345 us
    reduce_scatter x6, waiting for transfers between devices, own_block(): blocks = lax.psum_scatter(blocks, axes[k], scatter_dimension=0, tiled=True)  157 us
    all_gather x3, waiting for transfers between devices, broadcast(): lax.all_gather(shard, axis)  126 us
    all_gather x3, waiting for transfers between devices, stacked_from(): blocks = lax.all_gather(blocks, axes[k], axis=0, tiled=True)  119 us
    another operation x20, other arithmetic, on_device(): diagonal = jnp.linalg.cholesky(corner)  103 us
    unnamed x11, local copies, waits for them, and re-layouts  65.8 us
    another operation x7, other arithmetic, on_device(): lax.linalg.triangular_solve(diagonal, column, left_side=False, lower=True...  59.1 us
    reduce_sum x3, other arithmetic, spread(): jnp.sum(lax.all_gather(jnp.where(mine, shard, jnp.zeros_like(shard)), axi...  29.5 us
  transfers between devices with their start and end apart: 15, of which 15 were waited for; matrix products, arithmetic and copies ran while one was open for 0% of the time, Pallas kernels for 0%

profile of v1, /device:TPU:2, one launch (start us, length us, event | category | flops | bytes accessed | tf_op | source)
XLA Modules:
  0.0 1118.7 jit_solution(8118023325755052082)
XLA Ops:
  6.5 5.3 copy.36
  13.8 45.0 %all-gather.22.cloned.1.call-done = f32[4096,256]{0,1:T(8,128)} async-done(((f32[256,256]{0,1:T(8,128)}), f32[4096,256]{0,1:T(8,128)}) %all-gather.22.cloned.1.call-update) | async-done | bytes 4194320 | tf_op jit(solution)/shard_map/all_gather | solution.py:13
  60.9 11.7 %cholesky.172 = f32[128,128]{1,0:T(8,128)S(1)} custom-call(f32[128,128]{1,0:T(8,128)S(1)} %cholesky.270), custom_call_target="Cholesky" | custom-call | tf_op jit(solution)/shard_map/jit(cholesky)/cholesky | solution.py:76
  72.7 9.8 custom-call.15
  83.0 11.7 %cholesky.189 = f32[128,128]{1,0:T(8,128)S(1)} custom-call(f32[128,128]{1,0:T(8,128)S(1)} %convolution_subtract_fusion.8), custom_call_target="Cholesky" | custom-call | tf_op jit(solution)/shard_map/jit(cholesky)/cholesky | solution.py:76
  96.7 4.1 while.9
  100.8 19.7 %custom-call.16 = f32[2,128,128]{1,2,0:T(8,128)S(1)} custom-call(f32[2,128,128]{2,1,0:T(8,128)S(1)} %get-tuple-element.63), custom_call_target="InvertDiagBlocksLowerTriangular" | custom-call | tf_op jit(solution)/shard_map/triangular_solve/custom-call.0 | solution.py:77
  120.5 1.7 fusion.19
  126.3 115.0 %all-gather.24.cloned.1.call-done = f32[16384,256]{0,1:T(8,128)} async-done(((f32[1024,256]{0,1:T(8,128)}), f32[16384,256]{0,1:T(8,128)}) %all-gather.24.cloned.1.call-update) | async-done | bytes 16777232 | tf_op jit(solution)/shard_map/all_gather | solution.py:18
  241.3 18.6 %copy.66 = f32[32,8,16,1024]{3,2,1,0:T(8,128)} copy(f32[32,8,16,1024]{3,1,2,0:T(8,128)} %bitcast.152) | data formatting | bytes 33554432
  259.9 9.8 bitcast_reduce_fusion.2
  273.3 38.5 %reduce-scatter.7.cloned.1.call-done = f32[2,64,256]{2,1,0:T(8,128)} async-done(((f32[16,64,256]{2,1,0:T(8,128)}), f32[2,64,256]{2,1,0:T(8,128)}) %reduce-scatter.7.cloned.1.call-update) | async-done | bytes 131088 | tf_op jit(solution)/shard_map/reduce_scatter | solution.py:31
  311.8 13.9 %reduce-scatter.9.cloned.1.call-done = f32[1,64,256]{2,1,0:T(8,128)} async-done(((f32[2,64,256]{2,1,0:T(8,128)}), f32[1,64,256]{2,1,0:T(8,128)}) %reduce-scatter.9.cloned.1.call-update) | async-done | bytes 65552 | tf_op jit(solution)/shard_map/reduce_scatter | solution.py:31
  325.7 3.5 all_gather.58
  330.1 39.3 %all-gather.16.cloned.1.call-done = f32[16,64,256]{2,1,0:T(8,128)} async-done(((f32[2,64,256]{2,1,0:T(8,128)}), f32[16,64,256]{2,1,0:T(8,128)}) %all-gather.16.cloned.1.call-update) | async-done | bytes 1048592 | tf_op jit(solution)/shard_map/all_gather | solution.py:38
  371.0 5.5 convolution_subtract_fusion.2
  377.8 2.0 copy-done.1
  381.0 40.3 %all-gather.26.cloned.1.call-done = f32[4096,256]{0,1:T(8,128)} async-done(((f32[256,256]{0,1:T(8,128)}), f32[4096,256]{0,1:T(8,128)}) %all-gather.26.cloned.1.call-update) | async-done | bytes 4194320 | tf_op jit(solution)/shard_map/all_gather | solution.py:13
  423.4 11.7 %cholesky.206 = f32[128,128]{1,0:T(8,128)S(1)} custom-call(f32[128,128]{1,0:T(8,128)S(1)} %cholesky.273), custom_call_target="Cholesky" | custom-call | tf_op jit(solution)/shard_map/jit(cholesky)/cholesky | solution.py:76
  435.2 9.8 custom-call.17
  445.5 11.7 %cholesky.223 = f32[128,128]{1,0:T(8,128)S(1)} custom-call(f32[128,128]{1,0:T(8,128)S(1)} %convolution_subtract_fusion.7), custom_call_target="Cholesky" | custom-call | tf_op jit(solution)/shard_map/jit(cholesky)/cholesky | solution.py:76
  459.8 4.2 while.10
  464.0 19.7 %custom-call.18 = f32[2,128,128]{1,2,0:T(8,128)S(1)} custom-call(f32[2,128,128]{2,1,0:T(8,128)S(1)} %get-tuple-element.64), custom_call_target="InvertDiagBlocksLowerTriangular" | custom-call | tf_op jit(solution)/shard_map/triangular_solve/custom-call.0 | solution.py:77
  489.4 115.0 %all-gather.28.cloned.1.call-done = f32[16384,256]{0,1:T(8,128)} async-done(((f32[1024,256]{0,1:T(8,128)}), f32[16384,256]{0,1:T(8,128)}) %all-gather.28.cloned.1.call-update) | async-done | bytes 16777232 | tf_op jit(solution)/shard_map/all_gather | solution.py:18
  604.4 18.6 %copy.68 = f32[32,8,16,1024]{3,2,1,0:T(8,128)} copy(f32[32,8,16,1024]{3,1,2,0:T(8,128)} %bitcast.153) | data formatting | bytes 33554432
  623.0 9.8 bitcast_reduce_fusion.1
  636.4 38.5 %reduce-scatter.11.cloned.1.call-done = f32[2,64,256]{2,1,0:T(8,128)} async-done(((f32[16,64,256]{2,1,0:T(8,128)}), f32[2,64,256]{2,1,0:T(8,128)}) %reduce-scatter.11.cloned.1.call-update) | async-done | bytes 131088 | tf_op jit(solution)/shard_map/reduce_scatter | solution.py:31
  675.0 14.0 %reduce-scatter.13.cloned.1.call-done = f32[1,64,256]{2,1,0:T(8,128)} async-done(((f32[2,64,256]{2,1,0:T(8,128)}), f32[1,64,256]{2,1,0:T(8,128)}) %reduce-scatter.13.cloned.1.call-update) | async-done | bytes 65552 | tf_op jit(solution)/shard_map/reduce_scatter | solution.py:31
  689.0 3.5 all_gather.64
  692.7 39.9 %all-gather.18.cloned.1.call-done = f32[16,64,256]{2,1,0:T(8,128)} async-done(((f32[2,64,256]{2,1,0:T(8,128)}), f32[16,64,256]{2,1,0:T(8,128)}) %all-gather.18.cloned.1.call-update) | async-done | bytes 1048592 | tf_op jit(solution)/shard_map/all_gather | solution.py:38
  734.2 5.6 convolution_subtract_fusion.1
  741.2 2.0 copy-done
  744.3 40.5 %all-gather.30.cloned.1.call-done = f32[4096,256]{0,1:T(8,128)} async-done(((f32[256,256]{0,1:T(8,128)}), f32[4096,256]{0,1:T(8,128)}) %all-gather.30.cloned.1.call-update) | async-done | bytes 4194320 | tf_op jit(solution)/shard_map/all_gather | solution.py:13
  786.9 11.7 %cholesky.240 = f32[128,128]{1,0:T(8,128)S(1)} custom-call(f32[128,128]{1,0:T(8,128)S(1)} %cholesky.276), custom_call_target="Cholesky" | custom-call | tf_op jit(solution)/shard_map/jit(cholesky)/cholesky | solution.py:76
  798.7 9.8 custom-call.19
  809.0 11.7 %cholesky.257 = f32[128,128]{1,0:T(8,128)S(1)} custom-call(f32[128,128]{1,0:T(8,128)S(1)} %convolution_subtract_fusion.6), custom_call_target="Cholesky" | custom-call | tf_op jit(solution)/shard_map/jit(cholesky)/cholesky | solution.py:76
  823.2 4.0 while.11
  827.2 19.7 %custom-call.20 = f32[2,128,128]{1,2,0:T(8,128)S(1)} custom-call(f32[2,128,128]{2,1,0:T(8,128)S(1)} %get-tuple-element.65), custom_call_target="InvertDiagBlocksLowerTriangular" | custom-call | tf_op jit(solution)/shard_map/triangular_solve/custom-call.0 | solution.py:77
  852.7 115.0 %all-gather.32.cloned.1.call-done = f32[16384,256]{0,1:T(8,128)} async-done(((f32[1024,256]{0,1:T(8,128)}), f32[16384,256]{0,1:T(8,128)}) %all-gather.32.cloned.1.call-update) | async-done | bytes 16777232 | tf_op jit(solution)/shard_map/all_gather | solution.py:18
  967.6 18.6 %copy.70 = f32[32,8,16,1024]{3,2,1,0:T(8,128)} copy(f32[32,8,16,1024]{3,1,2,0:T(8,128)} %bitcast.154) | data formatting | bytes 33554432
  986.3 9.8 bitcast_reduce_fusion
  999.6 38.5 %reduce-scatter.15.cloned.1.call-done = f32[2,64,256]{2,1,0:T(8,128)} async-done(((f32[16,64,256]{2,1,0:T(8,128)}), f32[2,64,256]{2,1,0:T(8,128)}) %reduce-scatter.15.cloned.1.call-update) | async-done | bytes 131088 | tf_op jit(solution)/shard_map/reduce_scatter | solution.py:31
  1038.2 13.9 %reduce-scatter.17.cloned.1.call-done = f32[1,64,256]{2,1,0:T(8,128)} async-done(((f32[2,64,256]{2,1,0:T(8,128)}), f32[1,64,256]{2,1,0:T(8,128)}) %reduce-scatter.17.cloned.1.call-update) | async-done | bytes 65552 | tf_op jit(solution)/shard_map/reduce_scatter | solution.py:31
  1052.1 3.5 all_gather.70
  1055.8 40.0 %all-gather.20.cloned.1.call-done = f32[16,64,256]{2,1,0:T(8,128)} async-done(((f32[2,64,256]{2,1,0:T(8,128)}), f32[16,64,256]{2,1,0:T(8,128)}) %all-gather.20.cloned.1.call-update) | async-done | bytes 1048592 | tf_op jit(solution)/shard_map/all_gather | solution.py:38
  1097.3 5.7 convolution_subtract_fusion
  1103.9 2.4 select_bitcast_fusion
  1106.4 5.3 copy.58
  (168 shorter events, 62.3 us)
Async XLA Ops:
  6.5 52.3 %all-gather.22.cloned.1.call-start = ((), (), s32[]{:S(2)}) async-start(), calls=%async_computation.15 | async-start | bytes 4456448 | tf_op jit(solution)/shard_map/all_gather | solution.py:13
  13.6 227.7 %all-gather.24.cloned.1.call-start = ((), (), s32[]{:S(2)}) async-start(), calls=%async_computation.16 | async-start | bytes 17825792 | tf_op jit(solution)/shard_map/all_gather | solution.py:18
  126.2 185.5 %reduce-scatter.7.cloned.1.call-start = ((), (), s32[]{:S(2)}) async-start(), calls=%async_computation.6 | async-start | bytes 1179648 | tf_op jit(solution)/shard_map/reduce_scatter | solution.py:31
  273.2 52.5 %reduce-scatter.9.cloned.1.call-start = ((), (), s32[]{:S(2)}) async-start(), calls=%async_computation.7 | async-start | bytes 196608 | tf_op jit(solution)/shard_map/reduce_scatter | solution.py:31
  311.8 57.6 %all-gather.16.cloned.1.call-start = ((), (), s32[]{:S(2)}) async-start(), calls=%async_computation.8 | async-start | bytes 1179648 | tf_op jit(solution)/shard_map/all_gather | solution.py:38
  329.2 92.1 %all-gather.26.cloned.1.call-start = ((), (), s32[]{:S(2)}) async-start(), calls=%async_computation.17 | async-start | bytes 4456448 | tf_op jit(solution)/shard_map/all_gather | solution.py:13
  377.8 2.0 copy-start.1
  380.5 223.8 %all-gather.28.cloned.1.call-start = ((), (), s32[]{:S(2)}) async-start(), calls=%async_computation.18 | async-start | bytes 17825792 | tf_op jit(solution)/shard_map/all_gather | solution.py:18
  489.4 185.5 %reduce-scatter.11.cloned.1.call-start = ((), (), s32[]{:S(2)}) async-start(), calls=%async_computation.9 | async-start | bytes 1179648 | tf_op jit(solution)/shard_map/reduce_scatter | solution.py:31
  636.3 52.6 %reduce-scatter.13.cloned.1.call-start = ((), (), s32[]{:S(2)}) async-start(), calls=%async_computation.10 | async-start | bytes 196608 | tf_op jit(solution)/shard_map/reduce_scatter | solution.py:31
  674.9 57.8 %all-gather.18.cloned.1.call-start = ((), (), s32[]{:S(2)}) async-start(), calls=%async_computation.11 | async-start | bytes 1179648 | tf_op jit(solution)/shard_map/all_gather | solution.py:38
  692.5 92.3 %all-gather.30.cloned.1.call-start = ((), (), s32[]{:S(2)}) async-start(), calls=%async_computation.19 | async-start | bytes 4456448 | tf_op jit(solution)/shard_map/all_gather | solution.py:13
  741.2 2.0 copy-start
  744.0 223.6 %all-gather.32.cloned.1.call-start = ((), (), s32[]{:S(2)}) async-start(), calls=%async_computation.20 | async-start | bytes 17825792 | tf_op jit(solution)/shard_map/all_gather | solution.py:18
  852.6 185.5 %reduce-scatter.15.cloned.1.call-start = ((), (), s32[]{:S(2)}) async-start(), calls=%async_computation.12 | async-start | bytes 1179648 | tf_op jit(solution)/shard_map/reduce_scatter | solution.py:31
  999.6 52.5 %reduce-scatter.17.cloned.1.call-start = ((), (), s32[]{:S(2)}) async-start(), calls=%async_computation.13 | async-start | bytes 196608 | tf_op jit(solution)/shard_map/reduce_scatter | solution.py:31
  1038.2 57.6 %all-gather.20.cloned.1.call-start = ((), (), s32[]{:S(2)}) async-start(), calls=%async_computation.14 | async-start | bytes 1179648 | tf_op jit(solution)/shard_map/all_gather | solution.py:38
Sparse Core Ops, SparseCore 0:
  13.7 45.0 all-gather.21
  126.3 114.8 all-gather.23
  273.3 38.3 reduce-scatter.6
  314.1 11.5 reduce-scatter.8
  329.3 40.0 all-gather.15
  380.7 40.5 all-gather.25
  489.5 114.8 all-gather.27
  636.5 38.3 reduce-scatter.10
  677.3 11.5 reduce-scatter.12
  692.6 40.0 all-gather.17
  744.1 40.5 all-gather.29
  852.7 114.8 all-gather.31
  999.7 38.3 reduce-scatter.14
  1040.5 11.5 reduce-scatter.16
  1055.7 40.0 all-gather.19
